TPU v7x, 128 devices: a whole 4x4x4 slice. The times are simulated.
128 devices in a mesh: dp: 2 (over x_lo), phase: 16 (over z, y), tensor: 4 (over x_hi, core).
Axes of the slice: x: 4 (x_hi: 2, x_lo: 2; x = x_hi * 2 + x_lo), y: 4, z: 4, core: 2. Of those that a mesh axis runs over, the one named last changes fastest.
Arguments:
- tokens: bfloat16 [2, 2048, 8192], P('dp', 'phase', 'tensor'), may hold values from -6 to 6
- bc_proj: bfloat16 [2, 2048, 2, 2048], P('dp', 'phase', None, 'tensor'), may hold values from -0.3984375 to 0.3984375
- step_sizes: bfloat16 [2, 256, 1024], P('dp', 'phase', 'tensor'), may hold values from 0.5 to 2
- decay_rates: float32 [128], P('tensor'), may hold values from 6.1035156e-05 to 0.02
- direct_weight: float32 [128], P('tensor'), may hold values from 0.5 to 1.5
- norm_gain: float32 [8192], P('tensor'), may hold values from 0.1 to 1.9
- routes: int32 [2, 256, 1], P('dp', 'phase'), may hold values from 0 to 1; in each aligned block of 16 rows (0 to 15, 16 to 31, ..., all dimensions but the last counted through in order) at most 16 rows name the same one
- segments: int32 [2, 4096], P('dp', 'phase'), may hold values from 0 to 3, never falling along the last dimension, each value on 1 to 2048 neighbouring positions
Outputs:
- mixed: bfloat16 [2, 2048, 8192], P('dp', 'phase', 'tensor')
Inputs may be any that keep to these rules, and one draw needn't show every extreme that they name: `routes`: no device sends more than 16 of its blocks to one data group. `segments`: document ids never fall along a row; each document covers 1 to 2048 positions, and one covers exactly 2048.
All inputs are finite; a program needn't handle non-finite values.
Results may differ from a plain program's by a relative error of at most 0.0075.
Values may be sent and summed in bfloat16 or wider, within the bound.
No kernel may reach another device: no remote copies, remote signals or barrier semaphores. Data moves between devices by JAX's collectives and lax.ppermute only.
A program may use at most 128 MiB of HBM per device.

v0:
```python
import jax
import jax.numpy as jnp
from jax import lax
from jax.sharding import PartitionSpec as P

HEAD_FEATURES = 64
STATE_ENTRIES = 256
LOCAL_HEADS = 128
BLOCK = 8
EPSILON = 1e-05
PRECISE = lax.Precision.HIGHEST


def prefix(shard, axis, join, neutral):
    place = lax.axis_index(axis)
    gathered = jax.tree.map(
        lambda a, kind: lax.all_gather(a.astype(kind), axis),
        shard,
        (jnp.bfloat16, jnp.bfloat16, jnp.bfloat16, jnp.bfloat16),
    )
    state = jax.tree.map(lambda a, e: jnp.zeros_like(a) + jnp.asarray(e, a.dtype), shard, neutral)

    def one(step, state):
        return join(
            state,
            jax.tree.map(
                lambda a, own: lax.dynamic_index_in_dim(a, step, 0, False).astype(own.dtype),
                gathered,
                shard,
            ),
        )

    return lax.fori_loop(0, place, one, state)


def stretch_pass(
    carry_state, prior_id, x_stretch, b_stretch, c_stretch, dt_stretch, doc_ids, decay_rates
):
    span_len = x_stretch.shape[0]
    head_count = x_stretch.shape[1]
    groups = b_stretch.shape[1]
    per_group = head_count // groups
    log_decay = jnp.cumsum(-decay_rates[:, None] * dt_stretch, axis=1)
    x_groups = x_stretch.astype(jnp.float32).reshape(span_len, groups, per_group, -1)
    b_float = b_stretch.astype(jnp.float32)
    last_id = doc_ids[-1]
    tail_decay = (
        jnp.where(doc_ids[None, :] == last_id, jnp.exp(log_decay[:, -1:] - log_decay), 0.0)
        * dt_stretch
    )
    scaled = x_groups * tail_decay.T.reshape(span_len, groups, per_group)[..., None]
    update = jnp.einsum("jgkp,jgn->gkpn", scaled, b_float, precision=PRECISE).reshape(
        carry_state.shape
    )
    through = jnp.where(prior_id == last_id, jnp.exp(log_decay[:, -1]), 0.0)
    new_state = through[:, None, None] * carry_state + update
    positions = jnp.arange(span_len)
    same_doc = (doc_ids[:, None] == doc_ids[None, :]) & (positions[:, None] >= positions[None, :])
    gaps = jnp.minimum(log_decay[:, :, None] - log_decay[:, None, :], 0.0)
    decay_mat = jnp.where(same_doc[None], jnp.exp(gaps), 0.0) * dt_stretch[:, None, :]
    scores = jnp.einsum("ign,jgn->gij", c_stretch, b_stretch, preferred_element_type=jnp.float32)
    weights = decay_mat.reshape(groups, per_group, span_len, span_len) * scores[:, None]
    inside = jnp.einsum("gkij,jgkp->igkp", weights, x_groups, precision=PRECISE)
    state_groups = carry_state.reshape(
        groups, per_group, carry_state.shape[1], carry_state.shape[2]
    )
    carried = jnp.einsum(
        "ign,gkpn->igkp", c_stretch.astype(jnp.float32), state_groups, precision=PRECISE
    )
    keep_in = jnp.where(doc_ids[None, :] == prior_id, jnp.exp(log_decay), 0.0)
    result = inside + keep_in.T.reshape(span_len, groups, per_group)[..., None] * carried
    return (new_state, last_id, result.reshape(span_len, head_count, -1))


def local_scan(x_stretches, b_stretches, c_stretches, dt_stretches, doc_stretches, decay_rates):
    head_count = x_stretches.shape[2]

    def advance(carry, pieces):
        new_state, last_id, result = stretch_pass(
            carry[0], carry[1], pieces[0], pieces[1], pieces[2], pieces[3], pieces[4], decay_rates
        )
        return ((new_state, last_id), result)

    start_carry = (
        jnp.zeros((head_count, HEAD_FEATURES, STATE_ENTRIES), jnp.float32),
        jnp.array(-1.0, jnp.float32),
    )
    final_carry, scan_results = lax.scan(
        advance, start_carry, (x_stretches, b_stretches, c_stretches, dt_stretches, doc_stretches)
    )
    return (final_carry[0], scan_results)


def join_pieces(earlier, later):
    decay_one, state_one, first_one, last_one = earlier
    decay_two, state_two, first_two, last_two = later
    joined = (first_two == last_one) | (last_one < 0) | (first_two < 0)
    factor = jnp.where(joined, decay_two, 0.0)
    joined_state = factor[:, None, None] * state_one + state_two
    joined_decay = jnp.where(joined, decay_one * decay_two, 0.0)
    joined_first = jnp.where(first_one < 0, first_two, first_one)
    joined_last = jnp.where(last_two < 0, last_one, last_two)
    return (joined_decay, joined_state, joined_first, joined_last)


def per_device(
    tokens, bc_proj, step_sizes, decay_rates, direct_weight, norm_gain, routes, segments
):
    feature_width = tokens.shape[2]
    tok_count = tokens.shape[1]
    heads_dev = decay_rates.shape[0]
    groups_dev = bc_proj.shape[3] // STATE_ENTRIES
    per_group = heads_dev // groups_dev
    blocks = tok_count // BLOCK
    n_groups = lax.axis_size("dp")
    capacity = max(2, 2 * blocks // n_groups)
    slots = n_groups * capacity
    section = slots * BLOCK
    span_len = min(128, section)
    block_count = section // span_len
    targets = routes[0, :, 0]
    positions = jnp.arange(blocks)
    earlier = positions[:, None] > positions[None, :]
    slot_rank = jnp.sum((targets[:, None] == targets[None, :]) & earlier, axis=1)
    slot_index = targets * capacity + slot_rank
    placing = (slot_index[:, None] == jnp.arange(slots)[None, :]).astype(jnp.bfloat16)
    x_send = jnp.einsum(
        "bs,bf->sf",
        placing,
        tokens.reshape(blocks, BLOCK * feature_width),
        preferred_element_type=jnp.float32,
    )
    x_send = x_send.astype(jnp.bfloat16).reshape(n_groups, capacity, BLOCK, feature_width)
    bc_send = jnp.einsum(
        "bs,bf->sf",
        placing,
        bc_proj.reshape(blocks, BLOCK * 2 * groups_dev * STATE_ENTRIES),
        preferred_element_type=jnp.float32,
    )
    bc_send = bc_send.astype(jnp.bfloat16).reshape(
        n_groups, capacity, BLOCK, 2, groups_dev, STATE_ENTRIES
    )
    dt_send = jnp.einsum("bs,bf->sf", placing, step_sizes[0], preferred_element_type=jnp.float32)
    dt_send = dt_send.astype(jnp.bfloat16).reshape(n_groups, capacity, heads_dev * BLOCK)
    x_got, bc_got, dt_got = (
        lax.all_to_all(x_send, "dp", split_axis=0, concat_axis=0, tiled=True),
        lax.all_to_all(bc_send, "dp", split_axis=0, concat_axis=0, tiled=True),
        lax.all_to_all(dt_send, "dp", split_axis=0, concat_axis=0, tiled=True),
    )
    x_stretches = x_got.reshape(block_count, span_len, heads_dev, HEAD_FEATURES)
    b_stretches = bc_got[:, :, :, 0].reshape(block_count, span_len, groups_dev, STATE_ENTRIES)
    c_section = bc_got[:, :, :, 1].reshape(section, groups_dev, STATE_ENTRIES)
    c_stretches = c_section.reshape(block_count, span_len, groups_dev, STATE_ENTRIES)
    dt_section = (
        dt_got.reshape(slots, heads_dev, BLOCK)
        .astype(jnp.float32)
        .transpose(1, 0, 2)
        .reshape(heads_dev, section)
    )
    dt_stretches = dt_section.reshape(heads_dev, block_count, span_len).transpose(1, 0, 2)
    doc_ids = segments[0].astype(jnp.float32)
    doc_stretches = doc_ids.reshape(block_count, span_len)
    log_decay = jnp.cumsum(-decay_rates[:, None] * dt_section, axis=1)
    through = jnp.where(doc_ids[0] == doc_ids[-1], jnp.exp(log_decay[:, -1]), 0.0)
    identity = (
        jnp.ones((heads_dev,), jnp.float32),
        jnp.zeros((heads_dev, HEAD_FEATURES, STATE_ENTRIES), jnp.float32),
        jnp.array(-1.0, jnp.float32),
        jnp.array(-1.0, jnp.float32),
    )
    end_state, local_out = local_scan(
        x_stretches, b_stretches, c_stretches, dt_stretches, doc_stretches, decay_rates
    )
    incoming = prefix((through, end_state, doc_ids[0], doc_ids[-1]), "phase", join_pieces, identity)
    in_state = incoming[1]
    in_last = incoming[3]
    keep_in = jnp.where(doc_ids[None, :] == in_last, jnp.exp(log_decay), 0.0)
    state_groups = in_state.reshape(groups_dev, per_group, HEAD_FEATURES, STATE_ENTRIES)
    carried = jnp.einsum(
        "ign,gkpn->igkp", c_section.astype(jnp.float32), state_groups, precision=PRECISE
    )
    carried = carried.reshape(section, heads_dev, HEAD_FEATURES)
    combined = (
        local_out.reshape(section, heads_dev, HEAD_FEATURES) + keep_in.T[:, :, None] * carried
    )
    combined = combined + direct_weight[None, :, None] * x_got.reshape(
        section, heads_dev, HEAD_FEATURES
    ).astype(jnp.float32)
    y_section = combined.astype(jnp.bfloat16).reshape(section, feature_width)
    returned_rows = lax.all_to_all(
        y_section.reshape(n_groups, capacity, BLOCK * feature_width),
        "dp",
        split_axis=0,
        concat_axis=0,
        tiled=True,
    )
    restored = jnp.einsum(
        "bs,sf->bf",
        placing,
        returned_rows.reshape(slots, BLOCK * feature_width),
        preferred_element_type=jnp.float32,
    )
    restored = restored.astype(jnp.bfloat16).reshape(tok_count, feature_width)
    values = restored.astype(jnp.float32)
    square_sums = lax.psum(jnp.sum(values * values, axis=1), "tensor")
    mixed = (
        values
        * lax.rsqrt(square_sums / (LOCAL_HEADS * HEAD_FEATURES) + EPSILON)[:, None]
        * norm_gain
    ).astype(jnp.bfloat16)
    return mixed.reshape(1, tok_count, feature_width)


def solution(mesh):
    return jax.shard_map(
        per_device,
        mesh=mesh,
        in_specs=(
            P("dp", "phase", "tensor"),
            P("dp", "phase", None, "tensor"),
            P("dp", "phase", "tensor"),
            P("tensor"),
            P("tensor"),
            P("tensor"),
            P("dp", "phase", None),
            P("dp", "phase"),
        ),
        out_specs=P("dp", "phase", "tensor"),
        check_vma=False,
    )
```

profile of v0, /device:TPU:120, one launch (start us, length us, event | category | flops | bytes accessed | tf_op | source)
XLA Modules:
  0.0 328.3 jit_solution(4840087548735297066)
XLA Ops:
  6.5 0.9 convert_reduce_fusion
  7.5 0.7 multiply_add_fusion
  8.1 0.9 convolution_convert_fusion.3
  9.0 3.2 all-to-all-start
  12.2 1.1 reshape.293
  13.8 1.2 reshape.294
  15.2 0.9 all-to-all-done
  16.1 3.5 %all-to-all-start.2 = ((bf16[2,16,8,2,2,256]{5,4,3,2,1,0:T(2,128)(2,1)}), bf16[2,16,8,2,2,256]{5,4,3,2,1,0:T(2,128)(2,1)S(1)}, u32[]{:S(2)}, u32[]{:S(2)}) async-start(bf16[2,16,8,2,2,256]{5,4,3,2,1,0:T(2,128)(2,1)} %reshape.294), calls=%async_computation.2 | async-start | bytes 1048576 | tf_op jit(solution)/shard_map/all_to_all | solution.py:147
  20.1 1.6 copy.65
  21.7 5.2 %all-to-all-done.2 = bf16[2,16,8,2,2,256]{5,4,3,2,1,0:T(2,128)(2,1)S(1)} async-done(((bf16[2,16,8,2,2,256]{5,4,3,2,1,0:T(2,128)(2,1)}), bf16[2,16,8,2,2,256]{5,4,3,2,1,0:T(2,128)(2,1)S(1)}, u32[]{:S(2)}, u32[]{:S(2)}) %all-to-all-start.2) | async-done | bytes 524320 | tf_op jit(solution)/shard_map/all_to_all | solution.py:147
  26.9 3.6 %all-to-all-start.1 = ((bf16[2,16,8,2048]{3,2,1,0:T(8,128)(2,1)}), bf16[2,16,8,2048]{3,2,1,0:T(8,128)(2,1)S(1)}, u32[]{:S(2)}, u32[]{:S(2)}) async-start(bf16[2,16,8,2048]{3,2,1,0:T(8,128)(2,1)} %bitcast.66), calls=%async_computation.1 | async-start | bytes 2097152 | tf_op jit(solution)/shard_map/all_to_all | solution.py:146
  31.6 11.0 %all-to-all-done.1 = bf16[2,16,8,2048]{3,2,1,0:T(8,128)(2,1)S(1)} async-done(((bf16[2,16,8,2048]{3,2,1,0:T(8,128)(2,1)}), bf16[2,16,8,2048]{3,2,1,0:T(8,128)(2,1)S(1)}, u32[]{:S(2)}, u32[]{:S(2)}) %all-to-all-start.1) | async-done | bytes 1048608 | tf_op jit(solution)/shard_map/all_to_all | solution.py:146
  42.7 1.0 copy-done.4
  43.7 3.2 reshape.292
  46.9 3.3 %copy.54 = bf16[2,128,32,64]{1,3,2,0:T(8,128)(2,1)S(1)} copy(bf16[2,128,32,64]{3,2,1,0:T(8,128)(2,1)} %reshape.292) | data formatting | bytes 2097152
  50.2 25.7 %while.33 = (s32[]{:T(128)}, f32[32,64,256]{2,1,0:T(8,128)}, f32[]{:T(128)}, f32[2,128,32,64]{1,3,2,0:T(8,128)}, f32[2,128]{1,0:T(2,128)S(1)}, /*index=5*/f32[32...) while((s32[]{:T(128)}, f32[32,64,256]{2,1,0:T(8,128)}, ...), condition=%wide.region_3.4_spmd.clone, body=%wide.region_1.3_spmd.clone.sunk | while | flops 2035876096 | bytes 46125748 | solution.py:88
  50.2 0.8 slice.69
  52.3 1.0 fusion.81
  54.0 1.9 bitcast_add_fusion.2
  56.2 2.4 fusion.84
  58.6 1.1 fusion.85
  60.3 1.3 copy-done.8
  62.3 0.8 slice.69
  64.4 1.0 fusion.81
  66.0 3.5 %bitcast_add_fusion.2 = (f32[32,64,256]{2,1,0:T(8,128)}, f32[32,64,256]{2,1,0:T(8,128)S(1)}) fusion(f32[2,16,64,256]{3,2,1,0:T(8,128)S(1)} %fusion.81, f32[32]{0:T(128)S(1)} %broadcast_select_fusion.5, f32[32,64,256]{2,1,0:T(8,128)} %get-tuple-element.467, pred[]{:T(512)S(6)} %compare.3), kind=kLoop, calls=%fused_computation.3.clone.1 | loop fusion | flops 1572864 | bytes 8388737 | tf_op jit(solution)/shard_map/while/body/eval_jaxpr/add | solution.py:56
  69.8 2.4 fusion.84
  72.2 1.1 fusion.85
  73.9 1.3 copy-done.8
  75.9 2.7 convert_element_type.146
  81.7 0.6 dynamic-slice
  82.9 0.7 dynamic-update-slice
  83.7 0.8 dynamic-update-slice.2
  86.0 2.5 mul.184
  88.5 4.5 %mul.185 = f32[2,16,16384]{2,1,0:T(8,128)} reshape(f32[256,32,64]{2,1,0:T(8,128)} %mul.184) | data formatting | bytes 4194304 | tf_op jit(solution)/shard_map/mul | solution.py:186
  93.0 35.8 %all-reduce.3 = (bf16[16]{0:T(256)(128)(2,1)S(1)}, bf16[512]{0:T(512)(128)(2,1)S(1)}, bf16[16]{0:T(256)(128)(2,1)S(1)}) all-reduce(bf16[16]{0:T(256)(128)(2,1)S(1)} %dynamic-update-slice, bf16[512]{0:T(512)(128)(2,1)S(1)} %dynamic-update-slice.1, ...), channel_id=2, replica_groups=mesh['dp'=2,'phase'=16,'tensor'=4] {'phase'}, use_global_device_ids=true, to_apply=%add | all-reduce | flops 544 | bytes 2176 | tf_op jit(solution)/shard_map/all_gather | solution.py:17
  129.0 4.5 %copy.55 = f32[2,128,32,64]{3,2,1,0:T(8,128)} copy(f32[2,128,32,64]{1,3,2,0:T(8,128)S(1)} %copy-done.9) | data formatting | bytes 4194304 | tf_op jit(solution)/shard_map/while | solution.py:88
  133.5 4.1 %reshape.295 = f32[2,16,16384]{2,1,0:T(8,128)} reshape(f32[2,128,32,64]{3,2,1,0:T(8,128)} %copy.55) | data formatting | bytes 4194304 | tf_op jit(solution)/shard_map/reshape | solution.py:184
  137.6 1.6 reshape.304
  139.2 50.2 %all-gather.6.cloned.1.call-done = bf16[512,64,256]{2,1,0:T(8,128)(2,1)} async-done(((bf16[32,64,256]{2,1,0:T(8,128)(2,1)}), bf16[512,64,256]{2,1,0:T(8,128)(2,1)}) %all-gather.6.cloned.1.call-update) | async-done | bytes 16777232 | tf_op jit(solution)/shard_map/all_gather | solution.py:17
  189.6 82.4 %while.32 = (s32[]{:T(128)}, f32[32,64,256]{2,1,0:T(8,128)S(1)}, f32[]{:T(128)}, s32[]{:T(128)}, bf16[16]{0:T(256)(128)(2,1)S(1)}, /*index=5*/bf16[16,32]{1,0:T(...) while((s32[]{:T(128)}, f32[32,64,256]{2,1,0:T(8,128)S(1)}, ...), condition=%wide.region_7.8_spmd, body=%wide.region_6.7_spmd.sunk | while | flops 1572940 | bytes 5243423 | solution.py:33
  191.5 1.6 convert_add_fusion.2
  197.0 1.6 convert_add_fusion.2
  202.5 1.6 convert_add_fusion.2
  208.0 1.6 convert_add_fusion.2
  213.5 1.6 convert_add_fusion.2
  219.0 1.6 convert_add_fusion.2
  224.5 1.6 convert_add_fusion.2
  230.0 1.6 convert_add_fusion.2
  235.5 1.6 convert_add_fusion.2
  241.0 1.6 convert_add_fusion.2
  246.5 1.6 convert_add_fusion.2
  252.0 1.6 convert_add_fusion.2
  257.5 1.6 convert_add_fusion.2
  262.9 1.6 convert_add_fusion.2
  268.4 1.6 convert_add_fusion.2
  272.0 2.4 convolution_bitcast_fusion.1
  274.4 5.5 %copy.60 = f32[256,2,16,64]{3,2,1,0:T(8,128)} copy(f32[256,2,16,64]{0,3,2,1:T(8,128)} %convolution_bitcast_fusion.1) | data formatting | bytes 4194304 | tf_op jit(solution)/shard_map/ign,gkpn->igkp/transpose | solution.py:179
  280.0 3.9 %reshape.298 = f32[2,16,16384]{2,1,0:T(8,128)} reshape(f32[256,2,16,64]{3,2,1,0:T(8,128)} %copy.60) | data formatting | bytes 4194304 | tf_op jit(solution)/shard_map/reshape | solution.py:182
  284.0 2.6 mul.181
  286.6 4.0 %mul.182 = f32[2,16,16384]{2,1,0:T(8,128)} reshape(f32[256,32,64]{2,1,0:T(8,128)} %mul.181) | data formatting | bytes 4194304 | tf_op jit(solution)/shard_map/mul | solution.py:184
  290.6 4.2 %add_convert_fusion = bf16[2,16,16384]{2,1,0:T(8,128)(2,1)S(1)} fusion(f32[2,16,16384]{2,1,0:T(8,128)S(1)} %copy-done.6, f32[2,16,16384]{2,1,0:T(8,128)} %reshape.304, f32[2,16,16384]{2,1,0:T(8,128)} %reshape.295, f32[2,16,16384]{2,1,0:T(8,128)} %mul.182, f32[2,16,16384]{2,1,0:T(8,128)} %reshape.298), kind=kLoop, calls=%fused_computation.56 | loop fusion | flops 2621440 | bytes 11534336 | tf_op jit(solution)/shard_map/convert_element_type | solution.py:189
  294.8 16.2 %all_to_all.20 = bf16[2,16,16384]{2,1,0:T(8,128)(2,1)S(1)} all-to-all(bf16[2,16,16384]{2,1,0:T(8,128)(2,1)S(1)} %add_convert_fusion), channel_id=1, replica_groups=mesh['dp'=2,'phase'=16,'tensor'=4] {'dp'}, dimensions={0} | all-to-all | bytes 2097152 | tf_op jit(solution)/shard_map/all_to_all | solution.py:190
  311.7 8.5 %psum.7 = f32[128]{0:T(128)S(1)} all-reduce(f32[128]{0:T(128)S(1)} %reduce_sum.19), channel_id=1, replica_groups=mesh['dp'=2,'phase'=16,'tensor'=4] {'tensor'}, use_global_device_ids=true, to_apply=%region_9.10 | all-reduce | flops 128 | bytes 1024 | tf_op jit(solution)/shard_map/psum | solution.py:205
  320.5 0.9 multiply_convert_fusion
  (147 shorter events, 27.8 us)
Async XLA Ops:
  6.5 1.6 copy-start
  6.5 8.4 %copy-start.12 = (bf16[1,128,2048]{2,1,0:T(8,128)(2,1)S(1)}, bf16[1,128,2048]{2,1,0:T(8,128)(2,1)}, u32[]{:S(2)}) copy-start(bf16[1,128,2048]{2,1,0:T(8,128)(2,1)} %param.12) | copy-start | bytes 1572868
  9.0 7.1 %all-to-all-start = ((bf16[2,16,256]{2,1,0:T(8,128)(2,1)}), bf16[2,16,256]{2,1,0:T(8,128)(2,1)S(1)}, u32[]{:S(2)}, u32[]{:S(2)}) async-start(bf16[2,16,256]{2,1,0:T(8,128)(2,1)} %bitcast.9), calls=%async_computation | async-start | bytes 32768 | tf_op jit(solution)/shard_map/all_to_all | solution.py:148
  16.1 10.9 %all-to-all-start.2 = ((bf16[2,16,8,2,2,256]{5,4,3,2,1,0:T(2,128)(2,1)}), bf16[2,16,8,2,2,256]{5,4,3,2,1,0:T(2,128)(2,1)S(1)}, u32[]{:S(2)}, u32[]{:S(2)}) async-start(bf16[2,16,8,2,2,256]{5,4,3,2,1,0:T(2,128)(2,1)} %reshape.294), calls=%async_computation.2 | async-start | bytes 1048576 | tf_op jit(solution)/shard_map/all_to_all | solution.py:147
  20.1 10.5 %copy-start.16 = (f32[32]{0:T(128)S(1)}, f32[32]{0:T(128)}, u32[]{:S(2)}) copy-start(f32[32]{0:T(128)} %param.15) | copy-start | bytes 388
  20.1 10.5 %copy-start.14 = (s32[1,256]{1,0:T(1,128)S(1)}, s32[1,256]{1,0:T(1,128)}, u32[]{:S(2)}) copy-start(s32[1,256]{1,0:T(1,128)} %param.19) | copy-start | bytes 3076
  26.9 15.7 %all-to-all-start.1 = ((bf16[2,16,8,2048]{3,2,1,0:T(8,128)(2,1)}), bf16[2,16,8,2048]{3,2,1,0:T(8,128)(2,1)S(1)}, u32[]{:S(2)}, u32[]{:S(2)}) async-start(bf16[2,16,8,2048]{3,2,1,0:T(8,128)(2,1)} %bitcast.66), calls=%async_computation.1 | async-start | bytes 2097152 | tf_op jit(solution)/shard_map/all_to_all | solution.py:146
  30.5 158.8 %all-gather.6.cloned.1.call-start = ((), (), s32[]{:S(2)}) async-start(), calls=%async_computation.4 | async-start | bytes 17825792 | tf_op jit(solution)/shard_map/all_gather | solution.py:17
  31.1 15.8 %copy-start.10 = (f32[32,32,8]{0,2,1:T(8,128)}, f32[32,32,8]{0,2,1:T(8,128)S(1)}, u32[]{:S(2)}) copy-start(f32[32,32,8]{0,2,1:T(8,128)S(1)} %copy.50) | copy-start | bytes 98308
  42.7 1.1 copy-start.4
  50.2 2.1 copy-start.2
  58.6 1.6 copy-start.7
  59.7 1.9 copy-start.3
  60.3 1.3 copy-start.8
  62.3 2.1 copy-start.2
  72.2 1.6 copy-start.7
  73.4 1.9 copy-start.3
  73.9 1.3 copy-start.8
  75.9 5.8 %copy-start.17 = (u32[128]{0:T(128)S(1)}, u32[128]{0:T(128)}, u32[]{:S(2)}) copy-start(u32[128]{0:T(128)} %constant.87) | copy-start | bytes 1540
  75.9 8.6 %copy-start.11 = (f32[32,32,8]{0,2,1:T(8,128)S(1)}, f32[32,32,8]{0,2,1:T(8,128)}, u32[]{:S(2)}) copy-start(f32[32,32,8]{0,2,1:T(8,128)} %copy-done.10) | copy-start | bytes 98308
  75.9 10.0 %copy-start.15 = (f32[32]{0:T(128)S(1)}, f32[32]{0:T(128)}, u32[]{:S(2)}) copy-start(f32[32]{0:T(128)} %param.16) | copy-start | bytes 388
  88.5 40.5 %copy-start.9 = (f32[2,128,32,64]{1,3,2,0:T(8,128)S(1)}, f32[2,128,32,64]{1,3,2,0:T(8,128)}, u32[]{:S(2)}) copy-start(f32[2,128,32,64]{1,3,2,0:T(8,128)} %get-tuple-element.192) | copy-start | bytes 6291460
  133.5 4.1 %copy-start.5 = (bf16[2,16,8,2048]{3,2,1,0:T(8,128)(2,1)S(1)}, bf16[2,16,8,2048]{3,2,1,0:T(8,128)(2,1)}, u32[]{:S(2)}) copy-start(bf16[2,16,8,2048]{3,2,1,0:T(8,128)(2,1)} %copy-done.4) | copy-start | bytes 3145732
  286.6 4.0 %copy-start.6 = (f32[2,16,16384]{2,1,0:T(8,128)S(1)}, f32[2,16,16384]{2,1,0:T(8,128)}, u32[]{:S(2)}) copy-start(f32[2,16,16384]{2,1,0:T(8,128)} %mul.185) | copy-start | bytes 6291460
  311.6 8.9 %copy-start.13 = (f32[2048]{0:T(1024)S(1)}, f32[2048]{0:T(1024)}, u32[]{:S(2)}) copy-start(f32[2048]{0:T(1024)} %param.17) | copy-start | bytes 24580
  311.6 9.9 %copy-start.1 = (bf16[1,16,256]{2,1,0:T(8,128)(2,1)S(1)}, bf16[1,16,256]{2,1,0:T(8,128)(2,1)}, u32[]{:S(2)}) copy-start(bf16[1,16,256]{2,1,0:T(8,128)(2,1)} %param.14) | copy-start | bytes 24580
Sparse Core Ops, SparseCore 0:
  78.8 110.4 all-gather.5
where the time goes:
time: 330 us; the launch traced here: 328 us
  local copies, waits for them, and re-layouts  73.4 us (22%)
  waiting for transfers between devices  67.3 us (20%)
  blocking collectives  60.5 us (18%)
  other arithmetic  43.3 us (13%)
  loops' own time  42.7 us (13%)
  between operations  16.7 us (5%)
  matrix products  13.9 us (4%)
  starting transfers between devices  10.3 us (3%)
    all_gather x1, waiting for transfers between devices, prefix(): lax.all_gather(a.astype(kind), axis)  50.2 us
    another operation x1, loops' own time, prefix(): return lax.fori_loop(0, place, one, state)  39.9 us
    all_gather x1, blocking collectives, prefix(): lax.all_gather(a.astype(kind), axis)  35.8 us
    add x15, other arithmetic, join_pieces(): joined_state = factor[:, None, None] * state_one + state_two  24.7 us
    dynamic_slice x30, local copies, waits for them, and re-layouts, one(): lax.dynamic_index_in_dim(a, step, 0, False).astype(own.dtype)  17.7 us
    all_to_all x1, blocking collectives, per_device(): lax.all_to_all(y_section.reshape(n_groups, capacity, BLOCK * feature_widt...  16.2 us
    all_to_all x1, waiting for transfers between devices, per_device(): lax.all_to_all(x_send, 'dp', split_axis=0, concat_axis=0, tiled=True)  11 us
    psum x1, blocking collectives, per_device(): square_sums = lax.psum(jnp.sum(values * values, axis=1), 'tensor')  8.54 us
  transfers between devices with their start and end apart: 4, of which 4 were waited for; matrix products, arithmetic and copies ran while one was open for 8% of the time, Pallas kernels for 0%

commit v1 on v0

--- a/solution.py
+++ b/solution.py
@@ -1,3 +1,4 @@
+import functools
 import jax
 import jax.numpy as jnp
 from jax import lax
@@ -9,6 +10,13 @@
 BLOCK = 8
 EPSILON = 1e-05
 PRECISE = lax.Precision.HIGHEST
+
+
+def treat_slabs(original, link_axis):
+    return lax.all_gather(original, link_axis).sum(axis=0)
+
+
+choose_series = functools.partial(treat_slabs, link_axis="tensor")
 
 
 def prefix(shard, axis, join, neutral):
@@ -202,7 +210,7 @@
     )
     restored = restored.astype(jnp.bfloat16).reshape(tok_count, feature_width)
     values = restored.astype(jnp.float32)
-    square_sums = lax.psum(jnp.sum(values * values, axis=1), "tensor")
+    square_sums = choose_series(jnp.sum(values * values, axis=1))
     mixed = (
         values
         * lax.rsqrt(square_sums / (LOCAL_HEADS * HEAD_FEATURES) + EPSILON)[:, None]

time: 330 us -> 329 us (level)
    psum x1 -> x0, blocking collectives: 8.54 us -> none  [per_device(): square_sums = lax.psum(jnp.sum(values * values, axis=1), 'tensor')]
    all_gather x0 -> x1, blocking collectives: none -> 6.56 us  [treat_slabs(): return lax.all_gather(original, link_axis).sum(axis=0)]
where the time goes in v1:
time: 329 us; the launch traced here: 326 us
  local copies, waits for them, and re-layouts  73.4 us (22%)
  waiting for transfers between devices  67.3 us (20%)
  blocking collectives  58.6 us (18%)
  other arithmetic  43.3 us (13%)
  loops' own time  42.7 us (13%)
  between operations  16.7 us (5%)
  matrix products  13.9 us (4%)
  starting transfers between devices  10.3 us (3%)
    all_gather x1, waiting for transfers between devices, prefix(): lax.all_gather(a.astype(kind), axis)  50.2 us
    another operation x1, loops' own time, prefix(): return lax.fori_loop(0, place, one, state)  39.9 us
    all_gather x1, blocking collectives, prefix(): lax.all_gather(a.astype(kind), axis)  35.8 us
    add x15, other arithmetic, join_pieces(): joined_state = factor[:, None, None] * state_one + state_two  24.7 us
    dynamic_slice x30, local copies, waits for them, and re-layouts, one(): lax.dynamic_index_in_dim(a, step, 0, False).astype(own.dtype)  17.7 us
    all_to_all x1, blocking collectives, per_device(): lax.all_to_all(y_section.reshape(n_groups, capacity, BLOCK * feature_widt...  16.2 us
    all_to_all x1, waiting for transfers between devices, per_device(): lax.all_to_all(x_send, 'dp', split_axis=0, concat_axis=0, tiled=True)  11 us
    unnamed x38, local copies, waits for them, and re-layouts  8.53 us
  transfers between devices with their start and end apart: 4, of which 4 were waited for; matrix products, arithmetic and copies ran while one was open for 8% of the time, Pallas kernels for 0%

profile of v1, /device:TPU:120, one launch (start us, length us, event | category | flops | bytes accessed | tf_op | source)
XLA Modules:
  0.0 326.3 jit_solution(1781413549889477510)
XLA Ops:
  6.5 0.9 convert_reduce_fusion
  7.5 0.7 multiply_add_fusion
  8.1 0.9 convolution_convert_fusion.3
  9.0 3.2 all-to-all-start
  12.2 1.1 reshape.299
  13.8 1.2 reshape.300
  15.2 0.9 all-to-all-done
  16.1 3.5 %all-to-all-start.2 = ((bf16[2,16,8,2,2,256]{5,4,3,2,1,0:T(2,128)(2,1)}), bf16[2,16,8,2,2,256]{5,4,3,2,1,0:T(2,128)(2,1)S(1)}, u32[]{:S(2)}, u32[]{:S(2)}) async-start(bf16[2,16,8,2,2,256]{5,4,3,2,1,0:T(2,128)(2,1)} %reshape.300), calls=%async_computation.2 | async-start | bytes 1048576 | tf_op jit(solution)/shard_map/all_to_all | solution.py:155
  20.1 1.6 copy.65
  21.7 5.2 %all-to-all-done.2 = bf16[2,16,8,2,2,256]{5,4,3,2,1,0:T(2,128)(2,1)S(1)} async-done(((bf16[2,16,8,2,2,256]{5,4,3,2,1,0:T(2,128)(2,1)}), bf16[2,16,8,2,2,256]{5,4,3,2,1,0:T(2,128)(2,1)S(1)}, u32[]{:S(2)}, u32[]{:S(2)}) %all-to-all-start.2) | async-done | bytes 524320 | tf_op jit(solution)/shard_map/all_to_all | solution.py:155
  26.9 3.6 %all-to-all-start.1 = ((bf16[2,16,8,2048]{3,2,1,0:T(8,128)(2,1)}), bf16[2,16,8,2048]{3,2,1,0:T(8,128)(2,1)S(1)}, u32[]{:S(2)}, u32[]{:S(2)}) async-start(bf16[2,16,8,2048]{3,2,1,0:T(8,128)(2,1)} %bitcast.67), calls=%async_computation.1 | async-start | bytes 2097152 | tf_op jit(solution)/shard_map/all_to_all | solution.py:154
  31.6 11.0 %all-to-all-done.1 = bf16[2,16,8,2048]{3,2,1,0:T(8,128)(2,1)S(1)} async-done(((bf16[2,16,8,2048]{3,2,1,0:T(8,128)(2,1)}), bf16[2,16,8,2048]{3,2,1,0:T(8,128)(2,1)S(1)}, u32[]{:S(2)}, u32[]{:S(2)}) %all-to-all-start.1) | async-done | bytes 1048608 | tf_op jit(solution)/shard_map/all_to_all | solution.py:154
  42.7 1.0 copy-done.4
  43.7 3.2 reshape.298
  46.9 3.3 %copy.54 = bf16[2,128,32,64]{1,3,2,0:T(8,128)(2,1)S(1)} copy(bf16[2,128,32,64]{3,2,1,0:T(8,128)(2,1)} %reshape.298) | data formatting | bytes 2097152
  50.2 25.7 %while.33 = (s32[]{:T(128)}, f32[32,64,256]{2,1,0:T(8,128)}, f32[]{:T(128)}, f32[2,128,32,64]{1,3,2,0:T(8,128)}, f32[2,128]{1,0:T(2,128)S(1)}, /*index=5*/f32[32...) while((s32[]{:T(128)}, f32[32,64,256]{2,1,0:T(8,128)}, ...), condition=%wide.region_3.4_spmd.clone, body=%wide.region_1.3_spmd.clone.sunk | while | flops 2035876096 | bytes 46125748 | solution.py:96
  50.2 0.8 slice.69
  52.3 1.0 fusion.81
  54.0 1.9 bitcast_add_fusion.2
  56.2 2.4 fusion.84
  58.6 1.1 fusion.85
  60.3 1.3 copy-done.8
  62.3 0.8 slice.69
  64.4 1.0 fusion.81
  66.0 3.5 %bitcast_add_fusion.2 = (f32[32,64,256]{2,1,0:T(8,128)}, f32[32,64,256]{2,1,0:T(8,128)S(1)}) fusion(f32[2,16,64,256]{3,2,1,0:T(8,128)S(1)} %fusion.81, f32[32]{0:T(128)S(1)} %broadcast_select_fusion.5, f32[32,64,256]{2,1,0:T(8,128)} %get-tuple-element.467, pred[]{:T(512)S(6)} %compare.3), kind=kLoop, calls=%fused_computation.3.clone.1 | loop fusion | flops 1572864 | bytes 8388737 | tf_op jit(solution)/shard_map/while/body/eval_jaxpr/add | solution.py:64
  69.8 2.4 fusion.84
  72.2 1.1 fusion.85
  73.9 1.3 copy-done.8
  75.9 2.7 convert_element_type.146
  81.7 0.6 dynamic-slice
  82.9 0.7 dynamic-update-slice
  83.7 0.8 dynamic-update-slice.2
  86.0 2.5 mul.184
  88.5 4.5 %mul.185 = f32[2,16,16384]{2,1,0:T(8,128)} reshape(f32[256,32,64]{2,1,0:T(8,128)} %mul.184) | data formatting | bytes 4194304 | tf_op jit(solution)/shard_map/mul | solution.py:194
  93.0 35.8 %all-reduce.3 = (bf16[16]{0:T(256)(128)(2,1)S(1)}, bf16[512]{0:T(512)(128)(2,1)S(1)}, bf16[16]{0:T(256)(128)(2,1)S(1)}) all-reduce(bf16[16]{0:T(256)(128)(2,1)S(1)} %dynamic-update-slice, bf16[512]{0:T(512)(128)(2,1)S(1)} %dynamic-update-slice.1, ...), channel_id=2, replica_groups=mesh['dp'=2,'phase'=16,'tensor'=4] {'phase'}, use_global_device_ids=true, to_apply=%add | all-reduce | flops 544 | bytes 2176 | tf_op jit(solution)/shard_map/all_gather | solution.py:25
  129.0 4.5 %copy.55 = f32[2,128,32,64]{3,2,1,0:T(8,128)} copy(f32[2,128,32,64]{1,3,2,0:T(8,128)S(1)} %copy-done.9) | data formatting | bytes 4194304 | tf_op jit(solution)/shard_map/while | solution.py:96
  133.5 4.1 %reshape.301 = f32[2,16,16384]{2,1,0:T(8,128)} reshape(f32[2,128,32,64]{3,2,1,0:T(8,128)} %copy.55) | data formatting | bytes 4194304 | tf_op jit(solution)/shard_map/reshape | solution.py:192
  137.6 1.6 reshape.310
  139.2 50.2 %all-gather.8.cloned.1.call-done = bf16[512,64,256]{2,1,0:T(8,128)(2,1)} async-done(((bf16[32,64,256]{2,1,0:T(8,128)(2,1)}), bf16[512,64,256]{2,1,0:T(8,128)(2,1)}) %all-gather.8.cloned.1.call-update) | async-done | bytes 16777232 | tf_op jit(solution)/shard_map/all_gather | solution.py:25
  189.6 82.4 %while.32 = (s32[]{:T(128)}, f32[32,64,256]{2,1,0:T(8,128)S(1)}, f32[]{:T(128)}, s32[]{:T(128)}, bf16[16]{0:T(256)(128)(2,1)S(1)}, /*index=5*/bf16[16,32]{1,0:T(...) while((s32[]{:T(128)}, f32[32,64,256]{2,1,0:T(8,128)S(1)}, ...), condition=%wide.region_7.8_spmd, body=%wide.region_6.7_spmd.sunk | while | flops 1572940 | bytes 5243423 | solution.py:41
  191.5 1.6 convert_add_fusion.2
  197.0 1.6 convert_add_fusion.2
  202.5 1.6 convert_add_fusion.2
  208.0 1.6 convert_add_fusion.2
  213.5 1.6 convert_add_fusion.2
  219.0 1.6 convert_add_fusion.2
  224.5 1.6 convert_add_fusion.2
  230.0 1.6 convert_add_fusion.2
  235.5 1.6 convert_add_fusion.2
  241.0 1.6 convert_add_fusion.2
  246.5 1.6 convert_add_fusion.2
  252.0 1.6 convert_add_fusion.2
  257.5 1.6 convert_add_fusion.2
  262.9 1.6 convert_add_fusion.2
  268.4 1.6 convert_add_fusion.2
  272.0 2.4 convolution_bitcast_fusion.1
  274.4 5.5 %copy.60 = f32[256,2,16,64]{3,2,1,0:T(8,128)} copy(f32[256,2,16,64]{0,3,2,1:T(8,128)} %convolution_bitcast_fusion.1) | data formatting | bytes 4194304 | tf_op jit(solution)/shard_map/ign,gkpn->igkp/transpose | solution.py:187
  280.0 3.9 %reshape.304 = f32[2,16,16384]{2,1,0:T(8,128)} reshape(f32[256,2,16,64]{3,2,1,0:T(8,128)} %copy.60) | data formatting | bytes 4194304 | tf_op jit(solution)/shard_map/reshape | solution.py:190
  284.0 2.6 mul.181
  286.6 4.0 %mul.182 = f32[2,16,16384]{2,1,0:T(8,128)} reshape(f32[256,32,64]{2,1,0:T(8,128)} %mul.181) | data formatting | bytes 4194304 | tf_op jit(solution)/shard_map/mul | solution.py:192
  290.6 4.2 %add_convert_fusion = bf16[2,16,16384]{2,1,0:T(8,128)(2,1)S(1)} fusion(f32[2,16,16384]{2,1,0:T(8,128)S(1)} %copy-done.6, f32[2,16,16384]{2,1,0:T(8,128)} %reshape.310, f32[2,16,16384]{2,1,0:T(8,128)} %reshape.301, f32[2,16,16384]{2,1,0:T(8,128)} %mul.182, f32[2,16,16384]{2,1,0:T(8,128)} %reshape.304), kind=kLoop, calls=%fused_computation.56 | loop fusion | flops 2621440 | bytes 11534336 | tf_op jit(solution)/shard_map/convert_element_type | solution.py:197
  294.8 16.2 %all_to_all.20 = bf16[2,16,16384]{2,1,0:T(8,128)(2,1)S(1)} all-to-all(bf16[2,16,16384]{2,1,0:T(8,128)(2,1)S(1)} %add_convert_fusion), channel_id=1, replica_groups=mesh['dp'=2,'phase'=16,'tensor'=4] {'dp'}, dimensions={0} | all-to-all | bytes 2097152 | tf_op jit(solution)/shard_map/all_to_all | solution.py:198
  311.7 6.6 %all-gather.5 = f32[4,1,128]{2,1,0:T(1,128)S(1)} all-gather(f32[1,1,128]{2,1,0:T(1,128)S(1)} %bitcast.193), channel_id=6, replica_groups=mesh['dp'=2,'phase'=16,'tensor'=4] {'tensor'}, dimensions={0}, use_global_device_ids=true | all-gather | bytes 2560 | tf_op jit(solution)/shard_map/all_gather | solution.py:16
  318.5 0.9 multiply_convert_fusion
  (148 shorter events, 27.8 us)
Async XLA Ops:
  6.5 1.6 copy-start
  6.5 8.4 %copy-start.12 = (bf16[1,128,2048]{2,1,0:T(8,128)(2,1)S(1)}, bf16[1,128,2048]{2,1,0:T(8,128)(2,1)}, u32[]{:S(2)}) copy-start(bf16[1,128,2048]{2,1,0:T(8,128)(2,1)} %param.12) | copy-start | bytes 1572868
  9.0 7.1 %all-to-all-start = ((bf16[2,16,256]{2,1,0:T(8,128)(2,1)}), bf16[2,16,256]{2,1,0:T(8,128)(2,1)S(1)}, u32[]{:S(2)}, u32[]{:S(2)}) async-start(bf16[2,16,256]{2,1,0:T(8,128)(2,1)} %bitcast.9), calls=%async_computation | async-start | bytes 32768 | tf_op jit(solution)/shard_map/all_to_all | solution.py:156
  16.1 10.9 %all-to-all-start.2 = ((bf16[2,16,8,2,2,256]{5,4,3,2,1,0:T(2,128)(2,1)}), bf16[2,16,8,2,2,256]{5,4,3,2,1,0:T(2,128)(2,1)S(1)}, u32[]{:S(2)}, u32[]{:S(2)}) async-start(bf16[2,16,8,2,2,256]{5,4,3,2,1,0:T(2,128)(2,1)} %reshape.300), calls=%async_computation.2 | async-start | bytes 1048576 | tf_op jit(solution)/shard_map/all_to_all | solution.py:155
  20.1 10.5 %copy-start.16 = (f32[32]{0:T(128)S(1)}, f32[32]{0:T(128)}, u32[]{:S(2)}) copy-start(f32[32]{0:T(128)} %param.15) | copy-start | bytes 388
  20.1 10.5 %copy-start.14 = (s32[1,256]{1,0:T(1,128)S(1)}, s32[1,256]{1,0:T(1,128)}, u32[]{:S(2)}) copy-start(s32[1,256]{1,0:T(1,128)} %param.19) | copy-start | bytes 3076
  26.9 15.7 %all-to-all-start.1 = ((bf16[2,16,8,2048]{3,2,1,0:T(8,128)(2,1)}), bf16[2,16,8,2048]{3,2,1,0:T(8,128)(2,1)S(1)}, u32[]{:S(2)}, u32[]{:S(2)}) async-start(bf16[2,16,8,2048]{3,2,1,0:T(8,128)(2,1)} %bitcast.67), calls=%async_computation.1 | async-start | bytes 2097152 | tf_op jit(solution)/shard_map/all_to_all | solution.py:154
  30.5 158.8 %all-gather.8.cloned.1.call-start = ((), (), s32[]{:S(2)}) async-start(), calls=%async_computation.4 | async-start | bytes 17825792 | tf_op jit(solution)/shard_map/all_gather | solution.py:25
  31.1 15.8 %copy-start.10 = (f32[32,32,8]{0,2,1:T(8,128)}, f32[32,32,8]{0,2,1:T(8,128)S(1)}, u32[]{:S(2)}) copy-start(f32[32,32,8]{0,2,1:T(8,128)S(1)} %copy.50) | copy-start | bytes 98308
  42.7 1.1 copy-start.4
  50.2 2.1 copy-start.2
  58.6 1.6 copy-start.7
  59.7 1.9 copy-start.3
  60.3 1.3 copy-start.8
  62.3 2.1 copy-start.2
  72.2 1.6 copy-start.7
  73.4 1.9 copy-start.3
  73.9 1.3 copy-start.8
  75.9 5.8 %copy-start.17 = (u32[128]{0:T(128)S(1)}, u32[128]{0:T(128)}, u32[]{:S(2)}) copy-start(u32[128]{0:T(128)} %constant.87) | copy-start | bytes 1540
  75.9 8.6 %copy-start.11 = (f32[32,32,8]{0,2,1:T(8,128)S(1)}, f32[32,32,8]{0,2,1:T(8,128)}, u32[]{:S(2)}) copy-start(f32[32,32,8]{0,2,1:T(8,128)} %copy-done.10) | copy-start | bytes 98308
  75.9 10.0 %copy-start.15 = (f32[32]{0:T(128)S(1)}, f32[32]{0:T(128)}, u32[]{:S(2)}) copy-start(f32[32]{0:T(128)} %param.16) | copy-start | bytes 388
  88.5 40.5 %copy-start.9 = (f32[2,128,32,64]{1,3,2,0:T(8,128)S(1)}, f32[2,128,32,64]{1,3,2,0:T(8,128)}, u32[]{:S(2)}) copy-start(f32[2,128,32,64]{1,3,2,0:T(8,128)} %get-tuple-element.192) | copy-start | bytes 6291460
  133.5 4.1 %copy-start.5 = (bf16[2,16,8,2048]{3,2,1,0:T(8,128)(2,1)S(1)}, bf16[2,16,8,2048]{3,2,1,0:T(8,128)(2,1)}, u32[]{:S(2)}) copy-start(bf16[2,16,8,2048]{3,2,1,0:T(8,128)(2,1)} %copy-done.4) | copy-start | bytes 3145732
  286.6 4.0 %copy-start.6 = (f32[2,16,16384]{2,1,0:T(8,128)S(1)}, f32[2,16,16384]{2,1,0:T(8,128)}, u32[]{:S(2)}) copy-start(f32[2,16,16384]{2,1,0:T(8,128)} %mul.185) | copy-start | bytes 6291460
  311.6 7.0 %copy-start.13 = (f32[2048]{0:T(1024)S(1)}, f32[2048]{0:T(1024)}, u32[]{:S(2)}) copy-start(f32[2048]{0:T(1024)} %param.17) | copy-start | bytes 24580
  311.6 7.9 %copy-start.1 = (bf16[1,16,256]{2,1,0:T(8,128)(2,1)S(1)}, bf16[1,16,256]{2,1,0:T(8,128)(2,1)}, u32[]{:S(2)}) copy-start(bf16[1,16,256]{2,1,0:T(8,128)(2,1)} %param.14) | copy-start | bytes 24580
Sparse Core Ops, SparseCore 0:
  78.8 110.4 all-gather.7
